TPU v7x, 32 devices: a whole 2x2x4 slice. The times are simulated.
32 devices in a mesh: groups: 2 (over x), ep: 16 (over z, y, core).
Axes of the slice: x: 2, y: 2, z: 4, core: 2. Of those that a mesh axis runs over, the one named last changes fastest.
Arguments:
- states: float32 [2, 256, 2048], P(None, ('groups', 'ep')), parts along dimension 1, may hold values from -6 to 6
- attn_gain: float32 [2048], replicated, may hold values from 0.1 to 1.9
- moe_gain: float32 [2048], replicated, may hold values from 0.1 to 1.9
- w_query: bfloat16 [2048, 2048], P(None, 'ep'), may hold values from -11 to 11
- w_key: bfloat16 [2048, 256], P(None, 'ep'), may hold values from -0.125 to 0.125
- w_value: bfloat16 [2048, 256], P(None, 'ep'), may hold values from -0.125 to 0.125
- w_output: bfloat16 [2048, 2048], P('ep'), may hold values from -0.125 to 0.125
- w_gate_up: bfloat16 [16, 2048, 1536], P('ep'), may hold values from -0.125 to 0.125
- w_down: bfloat16 [16, 768, 2048], P('ep'), may hold values from -0.21875 to 0.21875
- key_cache: bfloat16 [64, 1024, 256], P(('groups', 'ep')), parts along dimension 0, may hold values from -60 to 60
- value_cache: bfloat16 [64, 1024, 256], P(('groups', 'ep')), parts along dimension 0, may hold values from -24 to 24
- cache_lengths: int32 [64], P(('groups', 'ep')), parts along dimension 0, may hold values from 1 to 1024, as said below
- prefix_slot: int32 [256], P(('groups', 'ep')), parts along dimension 0, may hold values from 0 to 1
- routes: int32 [256, 2, 8], P(('groups', 'ep')), parts along dimension 0, may hold values from 0 to 15, all different within a row; in each aligned block of 16 rows (0 to 15, 16 to 31, ..., all dimensions but the last counted through in order) at most 16 rows name the same one
- gate_weights: float32 [2, 256, 8], P(None, ('groups', 'ep')), parts along dimension 1, may hold values from 0.05 to 0.5
Outputs:
- layer_out: float32 [2, 256, 2048], P(None, ('groups', 'ep')), parts along dimension 1
- appended_kv: bfloat16 [2, 256, 512], P(None, ('groups', 'ep')), parts along dimension 1
There are 2 independent parts, one for each index of `groups`. A program takes and returns all parts, laid end to end along the dimension named above; an argument that names none is the same for every part. Nothing has to cross between parts.
Inputs may be any that keep to these rules, and one draw needn't show every extreme that they name: `cache_lengths`: positions beyond a prefix's length are unused; some prefix is full at 1024. `routes`: over both steps together, the 8 branches of one ep device choose any one expert at most 16 times; a branch's 8 experts at one step differ.
All inputs are finite; a program needn't handle non-finite values.
Results may differ from a plain program's by a relative error of at most 0.0024.
The roundings to bfloat16 on the way count: a program that leaves them out, or rounds other values in their place, can miss the bound.
Values may be sent and summed in bfloat16 or wider, within the bound.
A program may use at most 128 MiB of HBM per device.

v0:
```python
import math
import jax
import jax.numpy as jnp
from jax import lax
from jax.sharding import PartitionSpec as P

HQ = 16
KVH = 2
HD = 128
TOPK = 8
EPS = 1e-06
THETA = 1000000.0


def rms_scale(values, gain):
    squares = jnp.mean(values * values, axis=-1, keepdims=True)
    return values * lax.rsqrt(squares + EPS) * gain


def rotate(vectors, positions):
    head_size = vectors.shape[-1]
    half_size = head_size // 2
    inverse_rate = THETA ** (-(jnp.arange(half_size).astype(jnp.float32) * 2.0 / head_size))
    phases = positions[..., None, None] * inverse_rate
    cosine = jnp.cos(phases)
    sine_part = jnp.sin(phases)
    first_half = vectors[..., :half_size]
    second_half = vectors[..., half_size:]
    return jnp.concatenate(
        [
            first_half * cosine - second_half * sine_part,
            second_half * cosine + first_half * sine_part,
        ],
        axis=-1,
    )


def attend_block(queries, new_keys, new_values, key_block, value_block, lengths, slots):
    step_count, row_count, head_count, head_size = queries.shape
    prefix_count, cache_span, kv_heads, _ = key_block.shape
    group_size = head_count // kv_heads
    grouped = queries.reshape(step_count, row_count, kv_heads, group_size, head_size)
    inv_root = 1.0 / math.sqrt(head_size)
    far_scores = (
        jnp.einsum("srkgd,pckd->srkgpc", grouped, key_block, preferred_element_type=jnp.float32)
        * inv_root
    )
    visible = (jnp.arange(cache_span)[None, None, :] < lengths[None, :, None]) & (
        slots[:, None, None] == jnp.arange(prefix_count)[None, :, None]
    )
    far_scores = jnp.where(visible[None, :, None, None], far_scores, -1e30)
    own_scores = (
        jnp.einsum("srkgd,trkd->srkgt", grouped, new_keys, preferred_element_type=jnp.float32)
        * inv_root
    )
    causal = jnp.arange(step_count)[None, :] <= jnp.arange(step_count)[:, None]
    own_scores = jnp.where(causal[:, None, None, None, :], own_scores, -1e30)
    peak = jnp.maximum(jnp.max(far_scores, axis=(-2, -1)), jnp.max(own_scores, axis=-1))
    far_weights = jnp.exp(far_scores - peak[..., None, None])
    own_weights = jnp.exp(own_scores - peak[..., None])
    normalizer = jnp.sum(far_weights, axis=(-2, -1)) + jnp.sum(own_weights, axis=-1)
    far_probs = (far_weights / normalizer[..., None, None]).astype(jnp.bfloat16)
    own_probs = (own_weights / normalizer[..., None]).astype(jnp.bfloat16)
    attended = jnp.einsum(
        "srkgpc,pckd->srkgd", far_probs, value_block, preferred_element_type=jnp.float32
    )
    attended = attended + jnp.einsum(
        "srkgt,trkd->srkgd", own_probs, new_values, preferred_element_type=jnp.float32
    )
    return attended.reshape(step_count, row_count, head_count * head_size).astype(jnp.bfloat16)


def shards(
    states,
    attn_gain,
    moe_gain,
    w_query,
    w_key,
    w_value,
    w_output,
    w_gate_up,
    w_down,
    key_cache,
    value_cache,
    cache_lengths,
    prefix_slot,
    routes,
    gate_weights,
):
    devices = lax.axis_size("ep")
    step_count, row_count, model_width = states.shape
    query_cols = w_query.shape[1]
    kv_cols = w_key.shape[1]
    normed = rms_scale(states, attn_gain).astype(jnp.bfloat16)
    joined = jnp.concatenate([w_query, w_key, w_value], axis=1)
    head_parts = jnp.einsum(
        "srd,dc->src",
        lax.all_gather(normed, "ep", axis=1, tiled=True),
        joined,
        preferred_element_type=jnp.float32,
    )
    own_cols = lax.all_to_all(head_parts, "ep", split_axis=1, concat_axis=2, tiled=True)
    own_cols = own_cols.reshape(step_count, row_count, devices, query_cols + 2 * kv_cols)
    queries = own_cols[..., :query_cols].reshape(step_count, row_count, HQ, HD)
    new_keys = own_cols[..., query_cols : query_cols + kv_cols].reshape(
        step_count, row_count, KVH, HD
    )
    new_values = (
        own_cols[..., query_cols + kv_cols :]
        .reshape(step_count, row_count, KVH, HD)
        .astype(jnp.bfloat16)
    )
    prefix_count, cache_span, _ = key_cache.shape
    lengths_here = jnp.sum(
        jnp.where(
            prefix_slot[:, None] == jnp.arange(prefix_count)[None, :], cache_lengths[None, :], 0
        ),
        axis=1,
    )
    positions = (
        lengths_here.astype(jnp.float32)[None, :]
        + jnp.arange(step_count).astype(jnp.float32)[:, None]
    )
    queries = rotate(queries, positions).astype(jnp.bfloat16)
    new_keys = rotate(new_keys, positions).astype(jnp.bfloat16)
    attended = attend_block(
        queries,
        new_keys,
        new_values,
        key_cache.reshape(prefix_count, cache_span, KVH, HD),
        value_cache.reshape(prefix_count, cache_span, KVH, HD),
        cache_lengths,
        prefix_slot,
    )
    w_columns = lax.all_to_all(w_output, "ep", split_axis=1, concat_axis=0, tiled=True)
    column_part = jnp.einsum(
        "srf,fc->src",
        lax.all_gather(attended, "ep", axis=1, tiled=True),
        w_columns,
        preferred_element_type=jnp.float32,
    )
    projected = lax.all_to_all(column_part, "ep", split_axis=1, concat_axis=2, tiled=True)
    hidden = states + projected
    moe_input = (
        rms_scale(hidden, moe_gain)
        .astype(jnp.bfloat16)
        .reshape(step_count * row_count, model_width)
    )
    expert_count = w_gate_up.shape[0] * devices
    capacity = max(2, 4 * row_count * TOPK // expert_count)
    flat_routes = jnp.swapaxes(routes, 0, 1).reshape(-1)
    onehot = (flat_routes[:, None] == jnp.arange(expert_count)[None, :]).astype(jnp.int32)
    running = jnp.cumsum(onehot, axis=0) - 1
    within = jnp.sum(onehot * running, axis=1)
    slot_index = flat_routes * capacity + within
    dispatch = (jnp.arange(expert_count * capacity)[:, None] == slot_index[None, :]).astype(
        jnp.bfloat16
    )
    repeated = jnp.repeat(moe_input, TOPK, axis=0)
    outgoing = jnp.dot(dispatch, repeated, preferred_element_type=jnp.float32).astype(jnp.bfloat16)
    outgoing = outgoing.reshape(expert_count, capacity, model_width)
    both = jnp.einsum(
        "nsd,df->nsf",
        lax.all_to_all(outgoing, "ep", split_axis=0, concat_axis=0, tiled=True),
        w_gate_up[0],
        preferred_element_type=jnp.float32,
    )
    half_cols = both.shape[-1] // 2
    activation = (jax.nn.silu(both[..., :half_cols]) * both[..., half_cols:]).astype(jnp.bfloat16)
    expert_done = jnp.einsum(
        "nsf,fd->nsd", activation, w_down[0], preferred_element_type=jnp.float32
    ).astype(jnp.bfloat16)
    returned = lax.all_to_all(expert_done, "ep", split_axis=0, concat_axis=0, tiled=True)
    picked = returned.reshape(expert_count * capacity, model_width)[slot_index]
    picked = picked.astype(jnp.float32).reshape(step_count, row_count, TOPK, model_width)
    mixture = jnp.sum(gate_weights[..., None] * picked, axis=2)
    appended = jnp.concatenate(
        [
            new_keys.reshape(step_count, row_count, KVH * HD),
            new_values.reshape(step_count, row_count, KVH * HD),
        ],
        axis=-1,
    )
    return (hidden + mixture, appended)


def solution(mesh):
    return jax.shard_map(
        shards,
        mesh=mesh,
        in_specs=(
            P(None, ("groups", "ep"), None),
            P(),
            P(),
            P(None, "ep"),
            P(None, "ep"),
            P(None, "ep"),
            P("ep", None),
            P("ep", None, None),
            P("ep", None, None),
            P(("groups", "ep"), None, None),
            P(("groups", "ep"), None, None),
            P(("groups", "ep")),
            P(("groups", "ep")),
            P(("groups", "ep"), None, None),
            P(None, ("groups", "ep"), None),
        ),
        out_specs=(P(None, ("groups", "ep"), None), P(None, ("groups", "ep"), None)),
        check_vma=False,
    )
```

profile of v0, /device:TPU:9, one launch (start us, length us, event | category | flops | bytes accessed | tf_op | source)
XLA Modules:
  0.0 204.8 jit_solution(11933007128233373446)
XLA Ops:
  7.2 0.0 copy-start
  7.2 0.0 all-gather.3.cloned.1.call-start
  7.2 1.2 multiply_reduce_fusion.1
  8.4 1.6 multiply_convert_fusion.1
  10.0 0.0 all-gather.3.cloned.1.call-update
  10.0 2.0 copy.137
  12.1 0.9 select_reduce_fusion.1
  13.0 0.1 broadcast_add_fusion
  13.0 0.1 multiply_cosine_fusion
  13.2 2.2 %reshape.240 = bf16[2,1024,2,128]{3,2,1,0:T(2,128)(2,1)} reshape(bf16[2,1024,256]{2,1,0:T(8,128)(2,1)} %param.24) | data formatting | bytes 2097152 | tf_op jit(solution)/shard_map/reshape | solution.py:130
  15.5 2.1 %reshape.242 = bf16[2,1024,2,128]{3,2,1,0:T(2,128)(2,1)} reshape(bf16[2,1024,256]{2,1,0:T(8,128)(2,1)} %param.25) | data formatting | bytes 2097152 | tf_op jit(solution)/shard_map/reshape | solution.py:131
  17.6 0.1 iota_compare_fusion.4
  17.7 0.1 iota_compare_fusion.3
  17.8 31.6 %all-gather.3.cloned.1.call-done = bf16[2,128,2048]{2,1,0:T(8,128)(2,1)} async-done(((bf16[2,8,2048]{2,1,0:T(8,128)(2,1)}), bf16[2,128,2048]{2,1,0:T(8,128)(2,1)}) %all-gather.3.cloned.1.call-update) | async-done | bytes 1048592 | tf_op jit(solution)/shard_map/all_gather | solution.py:98
  49.4 1.9 fusion.19
  51.3 0.9 copy.138
  52.1 4.9 %all-to-all-start = ((f32[2,128,160]{2,0,1:T(2,128)}), f32[2,128,160]{2,0,1:T(2,128)S(1)}, u32[]{:S(2)}, u32[]{:S(2)}) async-start(f32[2,128,160]{2,0,1:T(2,128)} %copy.138), calls=%async_computation | async-start | bytes 524288 | tf_op jit(solution)/shard_map/all_to_all | solution.py:102
  57.0 0.0 all-gather.5.cloned.1.call-start
  57.1 0.5 iota_compare_fusion.5
  57.6 0.1 broadcast_and_fusion
  57.7 8.0 %all-to-all-done = f32[2,128,160]{2,0,1:T(2,128)S(1)} async-done(((f32[2,128,160]{2,0,1:T(2,128)}), f32[2,128,160]{2,0,1:T(2,128)S(1)}, u32[]{:S(2)}, u32[]{:S(2)}) %all-to-all-start) | async-done | bytes 163872 | tf_op jit(solution)/shard_map/all_to_all | solution.py:102
  65.8 0.1 subtract_convert_fusion
  65.9 0.1 slice.56
  66.0 0.1 reshape.241
  66.1 0.1 fusion.43
  66.3 0.1 maximum_convert_fusion
  66.4 1.1 fusion.44
  67.5 2.0 bitcast_reduce_fusion
  69.6 0.7 fusion.8
  70.2 0.1 fusion.33
  70.4 0.9 convolution_bitcast_fusion.1
  71.3 0.1 convert_element_type.86
  71.4 0.2 fusion.10
  71.6 0.7 convert_element_type.89
  72.3 0.0 all-gather.5.cloned.1.call-update
  72.3 2.0 copy_bitcast_fusion
  74.3 5.5 %all-to-all-start.1 = ((bf16[128,16,128]{2,0,1:T(8,128)(2,1)}), bf16[128,16,128]{2,0,1:T(8,128)(2,1)}, u32[]{:S(2)}, u32[]{:S(2)}) async-start(bf16[128,16,128]{2,0,1:T(8,128)(2,1)} %copy_bitcast_fusion), calls=%async_computation.1 | async-start | bytes 1048576 | tf_op jit(solution)/shard_map/all_to_all | solution.py:135
  79.8 0.1 reshape.243
  79.9 0.5 copy-done.5
  80.4 0.1 fusion.32
  80.5 0.2 reduce_window_sum.11
  80.7 15.2 %all-to-all-done.1 = bf16[128,16,128]{2,0,1:T(8,128)(2,1)} async-done(((bf16[128,16,128]{2,0,1:T(8,128)(2,1)}), bf16[128,16,128]{2,0,1:T(8,128)(2,1)}, u32[]{:S(2)}, u32[]{:S(2)}) %all-to-all-start.1) | async-done | bytes 524320 | tf_op jit(solution)/shard_map/all_to_all | solution.py:135
  95.9 15.3 %all-gather.5.cloned.1.call-done = bf16[2,128,2048]{2,1,0:T(8,128)(2,1)} async-done(((bf16[2,8,2048]{2,1,0:T(8,128)(2,1)}), bf16[2,128,2048]{2,1,0:T(8,128)(2,1)}) %all-gather.5.cloned.1.call-update) | async-done | bytes 1048592 | tf_op jit(solution)/shard_map/all_gather | solution.py:138
  111.3 1.8 fusion.45
  113.1 0.8 copy.161
  113.8 4.9 %all-to-all-start.2 = ((f32[2,128,128]{2,0,1:T(2,128)}), f32[2,128,128]{2,0,1:T(2,128)S(1)}, u32[]{:S(2)}, u32[]{:S(2)}) async-start(f32[2,128,128]{2,0,1:T(2,128)} %copy.161), calls=%async_computation.2 | async-start | bytes 262144 | tf_op jit(solution)/shard_map/all_to_all | solution.py:142
  118.7 0.8 select_reduce_fusion
  119.6 0.5 copy-done.6
  120.1 0.7 multiply_add_fusion.1
  120.7 3.9 %all-to-all-done.2 = f32[2,128,128]{2,0,1:T(2,128)S(1)} async-done(((f32[2,128,128]{2,0,1:T(2,128)}), f32[2,128,128]{2,0,1:T(2,128)S(1)}, u32[]{:S(2)}, u32[]{:S(2)}) %all-to-all-start.2) | async-done | bytes 131104 | tf_op jit(solution)/shard_map/all_to_all | solution.py:142
  124.6 0.1 multiply_reduce_fusion
  124.8 0.8 fusion.28
  125.5 0.4 convolution_convert_fusion
  126.0 30.0 %all_to_all.62 = bf16[16,16,2048]{2,1,0:T(8,128)(2,1)S(1)} all-to-all(bf16[16,16,2048]{2,1,0:T(8,128)(2,1)S(1)} %bitcast.120), channel_id=1, replica_groups=mesh['groups'=2,'ep'=16] {'ep'}, dimensions={0} | all-to-all | bytes 2097152 | tf_op jit(solution)/shard_map/all_to_all | solution.py:164
  156.0 4.6 %fusion = f32[16,16,1536]{2,1,0:T(8,128)S(1)} fusion(bf16[16,16,2048]{2,1,0:T(8,128)(2,1)S(1)} %all_to_all.62, bf16[1,2048,1536]{2,1,0:T(8,128)(2,1)} %param.22), kind=kOutput, calls=%fused_computation.1 | convolution fusion | flops 1610612736 | bytes 8912896 | tf_op jit(solution)/shard_map/nsd,df->nsf/dot_general | solution.py:162
  160.6 2.1 %fusion.4 = bf16[16,16,2048]{2,1,0:T(8,128)(2,1)} fusion(bf16[1,768,2048]{2,1,0:T(8,128)(2,1)S(1)} %copy-done, f32[16,16,1536]{2,1,0:T(8,128)S(1)} %fusion), kind=kOutput, calls=%fused_computation.6 | convolution fusion | flops 807010304 | bytes 5767168 | tf_op jit(solution)/shard_map/nsf,fd->nsd/dot_general | solution.py:170
  162.6 4.5 %all-to-all-start.4 = ((bf16[16,16,2048]{2,1,0:T(8,128)(2,1)}), bf16[16,16,2048]{2,1,0:T(8,128)(2,1)}, u32[]{:S(2)}, u32[]{:S(2)}) async-start(bf16[16,16,2048]{2,1,0:T(8,128)(2,1)} %fusion.4), calls=%async_computation.4 | async-start | bytes 2097152 | tf_op jit(solution)/shard_map/all_to_all | solution.py:173
  167.2 0.1 mul.221
  167.3 0.1 convert_element_type.98
  167.4 0.6 pad_maximum_fusion.1
  168.0 24.1 %all-to-all-done.4 = bf16[16,16,2048]{2,1,0:T(8,128)(2,1)} async-done(((bf16[16,16,2048]{2,1,0:T(8,128)(2,1)}), bf16[16,16,2048]{2,1,0:T(8,128)(2,1)}, u32[]{:S(2)}, u32[]{:S(2)}) %all-to-all-start.4) | async-done | bytes 1048608 | tf_op jit(solution)/shard_map/all_to_all | solution.py:173
  192.1 3.6 %gather_fusion = bf16[128,2048]{1,0:T(8,128)(2,1)} fusion(bf16[256,2048]{1,0:T(8,128)(2,1)} %bitcast.33, s32[1024]{0:T(1024)S(1)} %pad_clamp_fusion), kind=kCustom, calls=%fused_computation | custom fusion | bytes 1049088 | tf_op jit(solution)/shard_map/gather | solution.py:174
  195.7 1.5 fusion.13
  197.2 0.7 fusion.42
  (45 shorter events, 0.3 us)
Async XLA Ops:
  7.2 153.4 %copy-start = (bf16[1,768,2048]{2,1,0:T(8,128)(2,1)S(1)}, bf16[1,768,2048]{2,1,0:T(8,128)(2,1)}, u32[]{:S(2)}) copy-start(bf16[1,768,2048]{2,1,0:T(8,128)(2,1)} %param.23) | copy-start | bytes 9437188
  7.2 42.2 %all-gather.3.cloned.1.call-start = ((), (), s32[]{:S(2)}) async-start(), calls=%async_computation.5 | async-start | bytes 1114112 | tf_op jit(solution)/shard_map/all_gather | solution.py:98
  13.2 4.4 %copy-start.11 = (s32[8]{0:T(128)S(1)}, s32[8]{0:T(128)}, u32[]{:S(2)}) copy-start(s32[8]{0:T(128)} %param.27) | copy-start | bytes 100
  13.2 4.5 %copy-start.8 = (s32[2]{0:T(128)S(1)}, s32[2]{0:T(128)}, u32[]{:S(2)}) copy-start(s32[2]{0:T(128)} %param.26) | copy-start | bytes 28
  13.2 36.2 %copy-start.9 = (bf16[2048,16]{0,1:T(8,128)(2,1)S(1)}, bf16[2048,16]{0,1:T(8,128)(2,1)}, u32[]{:S(2)}) copy-start(bf16[2048,16]{0,1:T(8,128)(2,1)} %param.20) | copy-start | bytes 196612
  13.2 36.2 %copy-start.10 = (bf16[2048,16]{0,1:T(8,128)(2,1)S(1)}, bf16[2048,16]{0,1:T(8,128)(2,1)}, u32[]{:S(2)}) copy-start(bf16[2048,16]{0,1:T(8,128)(2,1)} %param.19) | copy-start | bytes 196612
  52.1 13.6 %all-to-all-start = ((f32[2,128,160]{2,0,1:T(2,128)}), f32[2,128,160]{2,0,1:T(2,128)S(1)}, u32[]{:S(2)}, u32[]{:S(2)}) async-start(f32[2,128,160]{2,0,1:T(2,128)} %copy.138), calls=%async_computation | async-start | bytes 524288 | tf_op jit(solution)/shard_map/all_to_all | solution.py:102
  57.0 54.2 %all-gather.5.cloned.1.call-start = ((), (), s32[]{:S(2)}) async-start(), calls=%async_computation.6 | async-start | bytes 1114112 | tf_op jit(solution)/shard_map/all_gather | solution.py:138
  67.5 2.8 %copy-start.2 = (bf16[2,1024,2,128]{3,2,1,0:T(2,128)(2,1)S(1)}, bf16[2,1024,2,128]{3,2,1,0:T(2,128)(2,1)}, u32[]{:S(2)}) copy-start(bf16[2,1024,2,128]{3,2,1,0:T(2,128)(2,1)} %reshape.242) | copy-start | bytes 3145732
  71.2 8.6 %copy-start.3 = (s32[8,2,8]{2,1,0:T(2,128)S(1)}, s32[8,2,8]{2,1,0:T(2,128)}, u32[]{:S(2)}) copy-start(s32[8,2,8]{2,1,0:T(2,128)} %param.28) | copy-start | bytes 1540
  72.3 52.3 %copy-start.1 = (f32[2,8,2048]{2,1,0:T(8,128)S(1)}, f32[2,8,2048]{2,1,0:T(8,128)}, u32[]{:S(2)}) copy-start(f32[2,8,2048]{2,1,0:T(8,128)} %param.15) | copy-start | bytes 393220
  74.3 21.6 %all-to-all-start.1 = ((bf16[128,16,128]{2,0,1:T(8,128)(2,1)}), bf16[128,16,128]{2,0,1:T(8,128)(2,1)}, u32[]{:S(2)}, u32[]{:S(2)}) async-start(bf16[128,16,128]{2,0,1:T(8,128)(2,1)} %copy_bitcast_fusion), calls=%async_computation.1 | async-start | bytes 1048576 | tf_op jit(solution)/shard_map/all_to_all | solution.py:135
  79.9 0.5 copy-start.5
  113.8 10.8 %all-to-all-start.2 = ((f32[2,128,128]{2,0,1:T(2,128)}), f32[2,128,128]{2,0,1:T(2,128)S(1)}, u32[]{:S(2)}, u32[]{:S(2)}) async-start(f32[2,128,128]{2,0,1:T(2,128)} %copy.161), calls=%async_computation.2 | async-start | bytes 262144 | tf_op jit(solution)/shard_map/all_to_all | solution.py:142
  119.6 0.5 copy-start.6
  162.6 4.6 %copy-start.7 = (s32[128]{0:T(128)S(1)}, s32[128]{0:T(128)}, u32[]{:S(2)}) copy-start(s32[128]{0:T(128)} %copy-done.6) | copy-start | bytes 1540
  162.6 29.5 %all-to-all-start.4 = ((bf16[16,16,2048]{2,1,0:T(8,128)(2,1)}), bf16[16,16,2048]{2,1,0:T(8,128)(2,1)}, u32[]{:S(2)}, u32[]{:S(2)}) async-start(bf16[16,16,2048]{2,1,0:T(8,128)(2,1)} %fusion.4), calls=%async_computation.4 | async-start | bytes 2097152 | tf_op jit(solution)/shard_map/all_to_all | solution.py:173
  192.1 3.6 %copy-start.4 = (f32[2,8,8]{2,1,0:T(8,128)S(1)}, f32[2,8,8]{2,1,0:T(8,128)}, u32[]{:S(2)}) copy-start(f32[2,8,8]{2,1,0:T(8,128)} %param.29) | copy-start | bytes 1540
Sparse Core Ops, SparseCore 0:
  10.8 38.5 all-gather.2
  72.4 38.7 all-gather.4
where the time goes:
time: 206 us; the launch traced here: 205 us
  waiting for transfers between devices  98.3 us (48%)
  blocking collectives  30 us (15%)
  starting transfers between devices  19.9 us (10%)
  local copies, waits for them, and re-layouts  16.2 us (8%)
  matrix products  15 us (7%)
  between operations  14.4 us (7%)
  other arithmetic  11 us (5%)
    all_gather x1, waiting for transfers between devices, shards(): lax.all_gather(normed, 'ep', axis=1, tiled=True)  31.6 us
    all_to_all x1, blocking collectives, shards(): lax.all_to_all(outgoing, 'ep', split_axis=0, concat_axis=0, tiled=True)  30 us
    all_to_all x1, waiting for transfers between devices, shards(): lax.all_to_all(expert_done, 'ep', split_axis=0, concat_axis=0, tiled=True)  24.1 us
    all_gather x1, waiting for transfers between devices, shards(): lax.all_gather(attended, 'ep', axis=1, tiled=True)  15.3 us
    all_to_all x1, waiting for transfers between devices, shards(): lax.all_to_all(w_output, 'ep', split_axis=1, concat_axis=0, tiled=True)  15.2 us
    all_to_all x1, waiting for transfers between devices, shards(): lax.all_to_all(head_parts, 'ep', split_axis=1, concat_axis=2, tiled=True)  8.01 us
    all_to_all x1, starting transfers between devices, shards(): lax.all_to_all(w_output, 'ep', split_axis=1, concat_axis=0, tiled=True)  5.47 us
    all_to_all x1, starting transfers between devices, shards(): lax.all_to_all(column_part, 'ep', split_axis=1, concat_axis=2, tiled=True)  4.92 us
  transfers between devices with their start and end apart: 6, of which 6 were waited for; matrix products, arithmetic and copies ran while one was open for 6% of the time, Pallas kernels for 0%

commit v1 on v0

--- a/solution.py
+++ b/solution.py
@@ -10,6 +10,22 @@
 TOPK = 8
 EPS = 1e-06
 THETA = 1000000.0
+
+
+def gather_around(x, axis, dim):
+    ways, here, hop = (lax.axis_size(axis), lax.axis_index(axis), x.shape[dim])
+    lengths = [n * ways if d == dim else n for d, n in enumerate(x.shape)]
+    full = lax.dynamic_update_slice_in_dim(jnp.zeros(lengths, x.dtype), x, here * hop, axis=dim)
+    going_up = going_down = x
+    for far in range(1, ways // 2 + 1):
+        going_up = lax.ppermute(going_up, axis, [(d, (d + 1) % ways) for d in range(ways)])
+        full = lax.dynamic_update_slice_in_dim(full, going_up, (here - far) % ways * hop, axis=dim)
+        if 2 * far < ways:
+            going_down = lax.ppermute(going_down, axis, [(d, (d - 1) % ways) for d in range(ways)])
+            full = lax.dynamic_update_slice_in_dim(
+                full, going_down, (here + far) % ways * hop, axis=dim
+            )
+    return full
 
 
 def rms_scale(values, gain):
@@ -135,7 +151,7 @@
     w_columns = lax.all_to_all(w_output, "ep", split_axis=1, concat_axis=0, tiled=True)
     column_part = jnp.einsum(
         "srf,fc->src",
-        lax.all_gather(attended, "ep", axis=1, tiled=True),
+        gather_around(attended, "ep", 1),
         w_columns,
         preferred_element_type=jnp.float32,
     )

time: 206 us -> 225 us (1.092)
  starting transfers between devices: 19.9 us -> 51.4 us
  waiting for transfers between devices: 98.3 us -> 72.4 us
  local copies, waits for them, and re-layouts: 16.2 us -> 27.5 us
    all_to_all x1, starting transfers between devices: 4.92 us -> 21.3 us  [shards(): lax.all_to_all(column_part, 'ep', split_axis=1, concat_axis=2, tiled=True)]
    all_gather x1 -> x0, waiting for transfers between devices: 15.3 us -> none  [shards(): lax.all_gather(attended, 'ep', axis=1, tiled=True)]
    all_to_all x1, waiting for transfers between devices: 15.2 us -> 0.01 us  [shards(): lax.all_to_all(w_output, 'ep', split_axis=1, concat_axis=0, tiled=True)]
    ppermute x0 -> x15, starting transfers between devices: none -> 15.2 us  [the longest x8 10.7 us: gather_around(): lax.ppermute(going_up, axis, [(d, (d + 1) % ways) for d in range(ways)])]
    dynamic_update_slice x0 -> x16, local copies, waits for them, and re-layouts: none -> 10.1 us  [the longest x8 5.03 us: gather_around(): lax.dynamic_update_slice_in_dim(full, going_up, (here - far) % ways * hop...]
    ppermute x0 -> x15, waiting for transfers between devices: none -> 7.91 us  [the longest x7 5.6 us: gather_around(): lax.ppermute(going_down, axis, [(d, (d - 1) % ways) for d in range(ways)])]
  transfers between devices with their start and end apart: 6 -> 20, of which waited for: 6 -> 11; matrix products, arithmetic and copies ran while one was open for 6% -> 15% of each run, Pallas kernels for 0% -> 0%
where the time goes in v1:
time: 225 us; the launch traced here: 224 us
  waiting for transfers between devices  72.4 us (32%)
  starting transfers between devices  51.4 us (23%)
  blocking collectives  30 us (13%)
  local copies, waits for them, and re-layouts  27.5 us (12%)
  matrix products  16.5 us (7%)
  between operations  14.7 us (7%)
  other arithmetic  11.8 us (5%)
    all_gather x1, waiting for transfers between devices, shards(): lax.all_gather(normed, 'ep', axis=1, tiled=True)  30.3 us
    all_to_all x1, blocking collectives, shards(): lax.all_to_all(outgoing, 'ep', split_axis=0, concat_axis=0, tiled=True)  30 us
    all_to_all x1, waiting for transfers between devices, shards(): lax.all_to_all(expert_done, 'ep', split_axis=0, concat_axis=0, tiled=True)  24.1 us
    all_to_all x1, starting transfers between devices, shards(): lax.all_to_all(column_part, 'ep', split_axis=1, concat_axis=2, tiled=True)  21.3 us
    ppermute x8, starting transfers between devices, gather_around(): lax.ppermute(going_up, axis, [(d, (d + 1) % ways) for d in range(ways)])  10.7 us
    all_to_all x1, waiting for transfers between devices, shards(): lax.all_to_all(head_parts, 'ep', split_axis=1, concat_axis=2, tiled=True)  6.19 us
    ppermute x7, waiting for transfers between devices, gather_around(): lax.ppermute(going_down, axis, [(d, (d - 1) % ways) for d in range(ways)])  5.6 us
    all_to_all x1, starting transfers between devices, shards(): lax.all_to_all(w_output, 'ep', split_axis=1, concat_axis=0, tiled=True)  5.46 us
  transfers between devices with their start and end apart: 20, of which 11 were waited for; matrix products, arithmetic and copies ran while one was open for 15% of the time, Pallas kernels for 0%

profile of v1, /device:TPU:9, one launch (start us, length us, event | category | flops | bytes accessed | tf_op | source)
XLA Modules:
  0.0 224.3 jit_solution(5724512397287458338)
XLA Ops:
  7.2 1.2 multiply_reduce_fusion.1
  8.4 1.6 multiply_convert_fusion.1
  10.3 2.1 copy.137
  12.3 0.9 select_reduce_fusion.1
  14.0 2.2 reshape.240
  16.3 2.1 reshape.242
  19.1 30.3 %all-gather.2.cloned.1.call-done = bf16[2,128,2048]{2,1,0:T(8,128)(2,1)} async-done(((bf16[2,8,2048]{2,1,0:T(8,128)(2,1)}), bf16[2,128,2048]{2,1,0:T(8,128)(2,1)}) %all-gather.2.cloned.1.call-update) | async-done | bytes 1048592 | tf_op jit(solution)/shard_map/all_gather | solution.py:114
  49.4 1.9 fusion.19
  51.3 0.8 copy.138
  52.1 4.9 %all-to-all-start = ((f32[2,128,160]{2,0,1:T(2,128)}), f32[2,128,160]{2,0,1:T(2,128)S(1)}, u32[]{:S(2)}, u32[]{:S(2)}) async-start(f32[2,128,160]{2,0,1:T(2,128)} %copy.138), calls=%async_computation | async-start | bytes 524288 | tf_op jit(solution)/shard_map/all_to_all | solution.py:118
  57.6 2.0 copy_bitcast_fusion
  59.5 6.2 %all-to-all-done = f32[2,128,160]{2,0,1:T(2,128)S(1)} async-done(((f32[2,128,160]{2,0,1:T(2,128)}), f32[2,128,160]{2,0,1:T(2,128)S(1)}, u32[]{:S(2)}, u32[]{:S(2)}) %all-to-all-start) | async-done | bytes 163872 | tf_op jit(solution)/shard_map/all_to_all | solution.py:118
  65.7 5.5 %all-to-all-start.1 = ((bf16[128,16,128]{2,0,1:T(8,128)(2,1)}), bf16[128,16,128]{2,0,1:T(8,128)(2,1)}, u32[]{:S(2)}, u32[]{:S(2)}) async-start(bf16[128,16,128]{2,0,1:T(8,128)(2,1)} %copy_bitcast_fusion), calls=%async_computation.1 | async-start | bytes 1048576 | tf_op jit(solution)/shard_map/all_to_all | solution.py:151
  71.3 0.7 slice.56
  72.3 0.7 multiply_subtract_fusion
  73.1 1.1 fusion.44
  74.3 2.0 bitcast_reduce_fusion
  76.4 0.7 fusion.8
  77.1 1.5 convolution_bitcast_fusion.1
  78.8 1.1 fusion.10
  80.0 1.5 collective-permute-start
  81.5 1.1 broadcast_in_dim.36
  82.6 0.6 constant_dynamic-update-slice_fusion.15
  83.3 1.9 collective-permute-start.2
  85.6 0.6 constant_dynamic-update-slice_fusion.14
  86.3 0.6 constant_dynamic-update-slice_fusion.13
  86.9 2.0 collective-permute-start.4
  88.9 0.9 collective-permute-done.3
  89.8 0.6 constant_dynamic-update-slice_fusion.12
  90.4 0.6 constant_dynamic-update-slice_fusion.11
  91.1 1.7 collective-permute-start.6
  92.8 1.4 collective-permute-done.5
  95.1 0.6 constant_dynamic-update-slice_fusion.9
  95.7 1.4 collective-permute-start.8
  97.2 1.5 collective-permute-done.7
  99.2 0.6 constant_dynamic-update-slice_fusion.8
  99.8 0.6 constant_dynamic-update-slice_fusion.7
  100.5 1.2 collective-permute-start.10
  101.7 0.7 collective-permute-done.9
  102.4 1.4 collective-permute-start.11
  103.8 0.6 constant_dynamic-update-slice_fusion.6
  104.4 0.6 constant_dynamic-update-slice_fusion.5
  105.5 0.7 collective-permute-done.11
  106.2 2.2 collective-permute-start.13
  108.4 0.6 constant_dynamic-update-slice_fusion.4
  109.0 0.6 constant_dynamic-update-slice_fusion.3
  110.1 0.6 constant_dynamic-update-slice_fusion.2
  110.8 0.6 constant_dynamic-update-slice_fusion.1
  111.4 2.3 %collective-permute-done.14 = bf16[2,8,2048]{2,1,0:T(8,128)(2,1)S(1)} collective-permute-done((bf16[2,8,2048]{2,1,0:T(8,128)(2,1)S(1)}, bf16[2,8,2048]{2,1,0:T(8,128)(2,1)S(1)}, u32[]{:S(2)}, u32[]{:S(2)}) %collective-permute-start.14) | collective-permute-done | bytes 65568 | tf_op jit(solution)/shard_map/ppermute | solution.py:21
  114.3 1.8 fusion.45
  116.1 0.8 copy.161
  116.9 21.3 %all-to-all-start.2 = ((f32[2,128,128]{2,0,1:T(2,128)}), f32[2,128,128]{2,0,1:T(2,128)S(1)}, u32[]{:S(2)}, u32[]{:S(2)}) async-start(f32[2,128,128]{2,0,1:T(2,128)} %copy.161), calls=%async_computation.2 | async-start | bytes 262144 | tf_op jit(solution)/shard_map/all_to_all | solution.py:158
  138.2 0.8 select_reduce_fusion
  139.6 0.7 multiply_add_fusion.1
  140.2 3.9 %all-to-all-done.2 = f32[2,128,128]{2,0,1:T(2,128)S(1)} async-done(((f32[2,128,128]{2,0,1:T(2,128)}), f32[2,128,128]{2,0,1:T(2,128)S(1)}, u32[]{:S(2)}, u32[]{:S(2)}) %all-to-all-start.2) | async-done | bytes 131104 | tf_op jit(solution)/shard_map/all_to_all | solution.py:158
  144.3 0.8 fusion.28
  145.5 30.0 %all_to_all.62 = bf16[16,16,2048]{2,1,0:T(8,128)(2,1)S(1)} all-to-all(bf16[16,16,2048]{2,1,0:T(8,128)(2,1)S(1)} %bitcast.120), channel_id=1, replica_groups=mesh['groups'=2,'ep'=16] {'ep'}, dimensions={0} | all-to-all | bytes 2097152 | tf_op jit(solution)/shard_map/all_to_all | solution.py:180
  175.5 4.6 %fusion = f32[16,16,1536]{2,1,0:T(8,128)S(1)} fusion(bf16[16,16,2048]{2,1,0:T(8,128)(2,1)S(1)} %all_to_all.62, bf16[1,2048,1536]{2,1,0:T(8,128)(2,1)} %param.22), kind=kOutput, calls=%fused_computation.1 | convolution fusion | flops 1610612736 | bytes 8912896 | tf_op jit(solution)/shard_map/nsd,df->nsf/dot_general | solution.py:178
  180.1 2.1 fusion.4
  182.1 4.5 %all-to-all-start.4 = ((bf16[16,16,2048]{2,1,0:T(8,128)(2,1)}), bf16[16,16,2048]{2,1,0:T(8,128)(2,1)}, u32[]{:S(2)}, u32[]{:S(2)}) async-start(bf16[16,16,2048]{2,1,0:T(8,128)(2,1)} %fusion.4), calls=%async_computation.4 | async-start | bytes 2097152 | tf_op jit(solution)/shard_map/all_to_all | solution.py:189
  187.5 24.1 %all-to-all-done.4 = bf16[16,16,2048]{2,1,0:T(8,128)(2,1)} async-done(((bf16[16,16,2048]{2,1,0:T(8,128)(2,1)}), bf16[16,16,2048]{2,1,0:T(8,128)(2,1)}, u32[]{:S(2)}, u32[]{:S(2)}) %all-to-all-start.4) | async-done | bytes 1048608 | tf_op jit(solution)/shard_map/all_to_all | solution.py:189
  211.6 3.6 %gather_fusion = bf16[128,2048]{1,0:T(8,128)(2,1)} fusion(bf16[256,2048]{1,0:T(8,128)(2,1)} %bitcast.33, s32[1024]{0:T(1024)S(1)} %pad_clamp_fusion), kind=kCustom, calls=%fused_computation | custom fusion | bytes 1049088 | tf_op jit(solution)/shard_map/gather | solution.py:190
  215.2 1.5 fusion.13
  216.8 0.7 fusion.42
  (89 shorter events, 8.2 us)
Async XLA Ops:
  7.2 172.9 %copy-start = (bf16[1,768,2048]{2,1,0:T(8,128)(2,1)S(1)}, bf16[1,768,2048]{2,1,0:T(8,128)(2,1)}, u32[]{:S(2)}) copy-start(bf16[1,768,2048]{2,1,0:T(8,128)(2,1)} %param.23) | copy-start | bytes 9437188
  7.2 42.2 %all-gather.2.cloned.1.call-start = ((), (), s32[]{:S(2)}) async-start(), calls=%async_computation.5 | async-start | bytes 1114112 | tf_op jit(solution)/shard_map/all_gather | solution.py:114
  14.0 4.4 %copy-start.4 = (s32[8,2,8]{2,1,0:T(2,128)S(1)}, s32[8,2,8]{2,1,0:T(2,128)}, u32[]{:S(2)}) copy-start(s32[8,2,8]{2,1,0:T(2,128)} %param.28) | copy-start | bytes 1540
  14.0 4.8 %copy-start.11 = (s32[8]{0:T(128)S(1)}, s32[8]{0:T(128)}, u32[]{:S(2)}) copy-start(s32[8]{0:T(128)} %param.27) | copy-start | bytes 100
  14.0 4.9 %copy-start.9 = (s32[2]{0:T(128)S(1)}, s32[2]{0:T(128)}, u32[]{:S(2)}) copy-start(s32[2]{0:T(128)} %param.26) | copy-start | bytes 28
  14.0 35.4 %copy-start.10 = (bf16[2048,16]{0,1:T(8,128)(2,1)S(1)}, bf16[2048,16]{0,1:T(8,128)(2,1)}, u32[]{:S(2)}) copy-start(bf16[2048,16]{0,1:T(8,128)(2,1)} %param.20) | copy-start | bytes 196612
  18.5 41.0 %copy-start.6 = (s32[128]{0:T(128)}, s32[128]{0:T(128)S(1)}, u32[]{:S(2)}) copy-start(s32[128]{0:T(128)S(1)} %reshape.243) | copy-start | bytes 1540
  52.1 13.6 %all-to-all-start = ((f32[2,128,160]{2,0,1:T(2,128)}), f32[2,128,160]{2,0,1:T(2,128)S(1)}, u32[]{:S(2)}, u32[]{:S(2)}) async-start(f32[2,128,160]{2,0,1:T(2,128)} %copy.138), calls=%async_computation | async-start | bytes 524288 | tf_op jit(solution)/shard_map/all_to_all | solution.py:118
  65.7 48.6 %all-to-all-start.1 = ((bf16[128,16,128]{2,0,1:T(8,128)(2,1)}), bf16[128,16,128]{2,0,1:T(8,128)(2,1)}, u32[]{:S(2)}, u32[]{:S(2)}) async-start(bf16[128,16,128]{2,0,1:T(8,128)(2,1)} %copy_bitcast_fusion), calls=%async_computation.1 | async-start | bytes 1048576 | tf_op jit(solution)/shard_map/all_to_all | solution.py:151
  74.3 2.8 %copy-start.2 = (bf16[2,1024,2,128]{3,2,1,0:T(2,128)(2,1)S(1)}, bf16[2,1024,2,128]{3,2,1,0:T(2,128)(2,1)}, u32[]{:S(2)}) copy-start(bf16[2,1024,2,128]{3,2,1,0:T(2,128)(2,1)} %reshape.242) | copy-start | bytes 3145732
  77.1 1.5 copy-start.3
  80.0 3.2 %collective-permute-start = (bf16[2,8,2048]{2,1,0:T(8,128)(2,1)S(1)}, bf16[2,8,2048]{2,1,0:T(8,128)(2,1)S(1)}, u32[]{:S(2)}, u32[]{:S(2)}) collective-permute-start(bf16[2,8,2048]{2,1,0:T(8,128)(2,1)S(1)} %convert_element_type.89), channel_id=1, source_target_pairs={{0,1},{1,2},{2,3},{3,4},{4,5},{5,6},{6,7},{7,8},{8,9},{9,10},{10,1... | collective-permute-start | bytes 196616 | tf_op jit(solution)/shard_map/ppermute | solution.py:21
  81.5 4.1 %collective-permute-start.1 = (bf16[2,8,2048]{2,1,0:T(8,128)(2,1)S(1)}, bf16[2,8,2048]{2,1,0:T(8,128)(2,1)S(1)}, u32[]{:S(2)}, u32[]{:S(2)}) collective-permute-start(bf16[2,8,2048]{2,1,0:T(8,128)(2,1)S(1)} %convert_element_type.89), channel_id=1, source_target_pairs={{0,15},{1,0},{2,1},{3,2},{4,3},{5,4},{6,5},{7,6},{8,7},{9,8},{10,9... | collective-permute-start | bytes 196616 | tf_op jit(solution)/shard_map/ppermute | solution.py:24
  83.3 3.7 %collective-permute-start.2 = (bf16[2,8,2048]{2,1,0:T(8,128)(2,1)S(1)}, bf16[2,8,2048]{2,1,0:T(8,128)(2,1)S(1)}, u32[]{:S(2)}, u32[]{:S(2)}) collective-permute-start(bf16[2,8,2048]{2,1,0:T(8,128)(2,1)S(1)} %collective-permute-done), channel_id=1, source_target_pairs={{0,1},{1,2},{2,3},{3,4},{4,5},{5,6},{6,7},{7,8},{8,9},{9,10},{10,1... | collective-permute-start | bytes 196616 | tf_op jit(solution)/shard_map/ppermute | solution.py:21
  85.6 4.1 %collective-permute-start.3 = (bf16[2,8,2048]{2,1,0:T(8,128)(2,1)S(1)}, bf16[2,8,2048]{2,1,0:T(8,128)(2,1)S(1)}, u32[]{:S(2)}, u32[]{:S(2)}) collective-permute-start(bf16[2,8,2048]{2,1,0:T(8,128)(2,1)S(1)} %collective-permute-done.1), channel_id=1, source_target_pairs={{0,15},{1,0},{2,1},{3,2},{4,3},{5,4},{6,5},{7,6},{8,7},{9,8},{10,9... | collective-permute-start | bytes 196616 | tf_op jit(solution)/shard_map/ppermute | solution.py:24
  86.3 57.9 %copy-start.1 = (f32[2,8,2048]{2,1,0:T(8,128)S(1)}, f32[2,8,2048]{2,1,0:T(8,128)}, u32[]{:S(2)}) copy-start(f32[2,8,2048]{2,1,0:T(8,128)} %param.15) | copy-start | bytes 393220
  86.9 4.1 %collective-permute-start.4 = (bf16[2,8,2048]{2,1,0:T(8,128)(2,1)S(1)}, bf16[2,8,2048]{2,1,0:T(8,128)(2,1)S(1)}, u32[]{:S(2)}, u32[]{:S(2)}) collective-permute-start(bf16[2,8,2048]{2,1,0:T(8,128)(2,1)S(1)} %collective-permute-done.2), channel_id=1, source_target_pairs={{0,1},{1,2},{2,3},{3,4},{4,5},{5,6},{6,7},{7,8},{8,9},{9,10},{10,1... | collective-permute-start | bytes 196616 | tf_op jit(solution)/shard_map/ppermute | solution.py:21
  89.7 4.4 %collective-permute-start.5 = (bf16[2,8,2048]{2,1,0:T(8,128)(2,1)S(1)}, bf16[2,8,2048]{2,1,0:T(8,128)(2,1)S(1)}, u32[]{:S(2)}, u32[]{:S(2)}) collective-permute-start(bf16[2,8,2048]{2,1,0:T(8,128)(2,1)S(1)} %collective-permute-done.3), channel_id=1, source_target_pairs={{0,15},{1,0},{2,1},{3,2},{4,3},{5,4},{6,5},{7,6},{8,7},{9,8},{10,9... | collective-permute-start | bytes 196616 | tf_op jit(solution)/shard_map/ppermute | solution.py:24
  91.1 4.7 %collective-permute-start.6 = (bf16[2,8,2048]{2,1,0:T(8,128)(2,1)S(1)}, bf16[2,8,2048]{2,1,0:T(8,128)(2,1)S(1)}, u32[]{:S(2)}, u32[]{:S(2)}) collective-permute-start(bf16[2,8,2048]{2,1,0:T(8,128)(2,1)S(1)} %collective-permute-done.4), channel_id=1, source_target_pairs={{0,1},{1,2},{2,3},{3,4},{4,5},{5,6},{6,7},{7,8},{8,9},{9,10},{10,1... | collective-permute-start | bytes 196616 | tf_op jit(solution)/shard_map/ppermute | solution.py:21
  94.1 4.5 %collective-permute-start.7 = (bf16[2,8,2048]{2,1,0:T(8,128)(2,1)S(1)}, bf16[2,8,2048]{2,1,0:T(8,128)(2,1)S(1)}, u32[]{:S(2)}, u32[]{:S(2)}) collective-permute-start(bf16[2,8,2048]{2,1,0:T(8,128)(2,1)S(1)} %collective-permute-done.5), channel_id=1, source_target_pairs={{0,15},{1,0},{2,1},{3,2},{4,3},{5,4},{6,5},{7,6},{8,7},{9,8},{10,9... | collective-permute-start | bytes 196616 | tf_op jit(solution)/shard_map/ppermute | solution.py:24
  95.7 4.7 %collective-permute-start.8 = (bf16[2,8,2048]{2,1,0:T(8,128)(2,1)S(1)}, bf16[2,8,2048]{2,1,0:T(8,128)(2,1)S(1)}, u32[]{:S(2)}, u32[]{:S(2)}) collective-permute-start(bf16[2,8,2048]{2,1,0:T(8,128)(2,1)S(1)} %collective-permute-done.6), channel_id=1, source_target_pairs={{0,1},{1,2},{2,3},{3,4},{4,5},{5,6},{6,7},{7,8},{8,9},{9,10},{10,1... | collective-permute-start | bytes 196616 | tf_op jit(solution)/shard_map/ppermute | solution.py:21
  98.7 3.7 %collective-permute-start.9 = (bf16[2,8,2048]{2,1,0:T(8,128)(2,1)S(1)}, bf16[2,8,2048]{2,1,0:T(8,128)(2,1)S(1)}, u32[]{:S(2)}, u32[]{:S(2)}) collective-permute-start(bf16[2,8,2048]{2,1,0:T(8,128)(2,1)S(1)} %collective-permute-done.7), channel_id=1, source_target_pairs={{0,15},{1,0},{2,1},{3,2},{4,3},{5,4},{6,5},{7,6},{8,7},{9,8},{10,9... | collective-permute-start | bytes 196616 | tf_op jit(solution)/shard_map/ppermute | solution.py:24
  100.5 4.6 %collective-permute-start.10 = (bf16[2,8,2048]{2,1,0:T(8,128)(2,1)S(1)}, bf16[2,8,2048]{2,1,0:T(8,128)(2,1)S(1)}, u32[]{:S(2)}, u32[]{:S(2)}) collective-permute-start(bf16[2,8,2048]{2,1,0:T(8,128)(2,1)S(1)} %collective-permute-done.8), channel_id=1, source_target_pairs={{0,1},{1,2},{2,3},{3,4},{4,5},{5,6},{6,7},{7,8},{8,9},{9,10},{10,1... | collective-permute-start | bytes 196616 | tf_op jit(solution)/shard_map/ppermute | solution.py:21
  102.4 3.8 %collective-permute-start.11 = (bf16[2,8,2048]{2,1,0:T(8,128)(2,1)S(1)}, bf16[2,8,2048]{2,1,0:T(8,128)(2,1)S(1)}, u32[]{:S(2)}, u32[]{:S(2)}) collective-permute-start(bf16[2,8,2048]{2,1,0:T(8,128)(2,1)S(1)} %collective-permute-done.9), channel_id=1, source_target_pairs={{0,15},{1,0},{2,1},{3,2},{4,3},{5,4},{6,5},{7,6},{8,7},{9,8},{10,9... | collective-permute-start | bytes 196616 | tf_op jit(solution)/shard_map/ppermute | solution.py:24
  105.0 4.6 %collective-permute-start.12 = (bf16[2,8,2048]{2,1,0:T(8,128)(2,1)S(1)}, bf16[2,8,2048]{2,1,0:T(8,128)(2,1)S(1)}, u32[]{:S(2)}, u32[]{:S(2)}) collective-permute-start(bf16[2,8,2048]{2,1,0:T(8,128)(2,1)S(1)} %collective-permute-done.10), channel_id=1, source_target_pairs={{0,1},{1,2},{2,3},{3,4},{4,5},{5,6},{6,7},{7,8},{8,9},{9,10},{10,1... | collective-permute-start | bytes 196616 | tf_op jit(solution)/shard_map/ppermute | solution.py:21
  106.2 4.6 %collective-permute-start.13 = (bf16[2,8,2048]{2,1,0:T(8,128)(2,1)S(1)}, bf16[2,8,2048]{2,1,0:T(8,128)(2,1)S(1)}, u32[]{:S(2)}, u32[]{:S(2)}) collective-permute-start(bf16[2,8,2048]{2,1,0:T(8,128)(2,1)S(1)} %collective-permute-done.11), channel_id=1, source_target_pairs={{0,15},{1,0},{2,1},{3,2},{4,3},{5,4},{6,5},{7,6},{8,7},{9,8},{10,9... | collective-permute-start | bytes 196616 | tf_op jit(solution)/shard_map/ppermute | solution.py:24
  109.6 4.1 %collective-permute-start.14 = (bf16[2,8,2048]{2,1,0:T(8,128)(2,1)S(1)}, bf16[2,8,2048]{2,1,0:T(8,128)(2,1)S(1)}, u32[]{:S(2)}, u32[]{:S(2)}) collective-permute-start(bf16[2,8,2048]{2,1,0:T(8,128)(2,1)S(1)} %collective-permute-done.12), channel_id=1, source_target_pairs={{0,1},{1,2},{2,3},{3,4},{4,5},{5,6},{6,7},{7,8},{8,9},{9,10},{10,1... | collective-permute-start | bytes 196616 | tf_op jit(solution)/shard_map/ppermute | solution.py:21
  116.9 27.3 %all-to-all-start.2 = ((f32[2,128,128]{2,0,1:T(2,128)}), f32[2,128,128]{2,0,1:T(2,128)S(1)}, u32[]{:S(2)}, u32[]{:S(2)}) async-start(f32[2,128,128]{2,0,1:T(2,128)} %copy.161), calls=%async_computation.2 | async-start | bytes 262144 | tf_op jit(solution)/shard_map/all_to_all | solution.py:158
  139.0 0.5 copy-start.7
  182.1 4.6 %copy-start.8 = (s32[128]{0:T(128)S(1)}, s32[128]{0:T(128)}, u32[]{:S(2)}) copy-start(s32[128]{0:T(128)} %copy-done.7) | copy-start | bytes 1540
  182.1 29.5 %all-to-all-start.4 = ((bf16[16,16,2048]{2,1,0:T(8,128)(2,1)}), bf16[16,16,2048]{2,1,0:T(8,128)(2,1)}, u32[]{:S(2)}, u32[]{:S(2)}) async-start(bf16[16,16,2048]{2,1,0:T(8,128)(2,1)} %fusion.4), calls=%async_computation.4 | async-start | bytes 2097152 | tf_op jit(solution)/shard_map/all_to_all | solution.py:189
  211.6 3.7 %copy-start.5 = (f32[2,8,8]{2,1,0:T(8,128)S(1)}, f32[2,8,8]{2,1,0:T(8,128)}, u32[]{:S(2)}) copy-start(f32[2,8,8]{2,1,0:T(8,128)} %param.29) | copy-start | bytes 1540
Sparse Core Ops, SparseCore 0:
  10.8 38.5 all-gather.1
